TPU v7x, 32 devices: a whole 2x2x4 slice. The times are simulated.
32 devices in a mesh: chan: 4 (over z), sub: 8 (over y, x, core).
Axes of the slice: x: 2, y: 2, z: 4, core: 2. Of those that a mesh axis runs over, the one named last changes fastest.
Arguments:
- visibilities: float32 [2, 64, 1024], P(None, 'sub', 'chan'), may hold values from -6 to 6
- uv_offset: float32 [2, 64, 1024], P(None, 'sub', 'chan'), may hold values from -9 to 9
- chan_index: int32 [64, 1024], P('sub', 'chan'), may hold values from 0 to 4095
- counts: int32 [64, 4], P('sub', 'chan'), may hold values from 1 to 256, as said below
- row_tile: int32 [64], P('sub'), may hold values from 0 to 7
- col_tile: int32 [64], P('sub'), may hold values from 0 to 63
- primary_beam: float32 [2048, 2048], P(('chan', 'sub')), may hold values from 0.2 to 1
- model_image: float32 [2048, 2048], P(('chan', 'sub')), may hold values from -3 to 3
Outputs:
- new_model: float32 [2048, 2048], P(('chan', 'sub'))
- predicted: float32 [2, 64, 1024], P(None, 'sub', 'chan')
Inputs may be any that keep to these rules, and one draw needn't show every extreme that they name: `counts`: the number of leading slots, of the 256 slots of a subgrid in a channel shard, that hold visibilities; later slots are padding and are ignored; some subgrid in some shard has all 256 slots filled.
All inputs are finite; a program needn't handle non-finite values.
Results may differ from a plain program's by a relative error of at most 0.0003.
Values sent between devices are 32-bit elements; how exact they have to be, the bound alone decides.
No kernel may reach another device: no remote copies, remote signals or barrier semaphores. Data moves between devices by JAX's collectives and lax.ppermute only.
A program may use at most 64 MiB of HBM per device.

v0:
```python
import functools
import math

import jax
import jax.numpy as jnp
import numpy as np
from jax import lax
from jax.experimental import pallas as pl
from jax.experimental.pallas import tpu as pltpu
from jax.sharding import PartitionSpec as P

SG = 32
CH_DEV = 4096
SUB_DEV = 8
CAP = 256
LANES = 128
RADIX = 16


precise = lax.Precision.HIGHEST


def complex_einsum(formula, left_re, left_im, right_re, right_im):
    if right_im is None:
        real_part = jnp.einsum(formula, left_re, right_re, precision=precise)
        imag_part = jnp.einsum(formula, left_im, right_re, precision=precise)
        return (real_part, imag_part)
    real_part = jnp.einsum(formula, left_re, right_re, precision=precise) - jnp.einsum(
        formula, left_im, right_im, precision=precise
    )
    imag_part = jnp.einsum(formula, left_re, right_im, precision=precise) + jnp.einsum(
        formula, left_im, right_re, precision=precise
    )
    return (real_part, imag_part)


def root_table(leading, trailing, modulus, polarity):
    first_index = jnp.arange(leading, dtype=jnp.int32)
    second_index = jnp.arange(trailing, dtype=jnp.int32)
    product = first_index[:, None] * second_index[None, :] % modulus
    phase_angle = polarity * 2.0 * math.pi / modulus * product.astype(jnp.float32)
    return (jnp.cos(phase_angle), jnp.sin(phase_angle))


def split_factor(extent):
    factor = math.isqrt(extent)
    while extent % factor:
        factor -= 1
    return factor


def transform_last(values_re, values_im, polarity):
    extent = values_re.shape[-1]
    inner_count = split_factor(extent)
    outer_count = extent // inner_count
    row_count = values_re.shape[0]
    shaped_re = values_re.reshape(row_count, outer_count, inner_count)
    shaped_im = (
        None if values_im is None else values_im.reshape(row_count, outer_count, inner_count)
    )
    outer_cos, outer_sin = root_table(outer_count, outer_count, outer_count, polarity)
    section_re, section_im = complex_einsum(
        "kn,rnm->rkm", outer_cos, outer_sin, shaped_re, shaped_im
    )
    twist_cos, twist_sin = root_table(outer_count, inner_count, extent, polarity)
    twisted_re = section_re * twist_cos - section_im * twist_sin
    twisted_im = section_re * twist_sin + section_im * twist_cos
    inner_cos, inner_sin = root_table(inner_count, inner_count, inner_count, polarity)
    result_re, result_im = complex_einsum(
        "jm,rkm->rjk", inner_cos, inner_sin, twisted_re, twisted_im
    )
    return (result_re.reshape(row_count, extent), result_im.reshape(row_count, extent))


def centred_table(polarity):
    counter = jnp.arange(SG, dtype=jnp.int32) - SG // 2
    product = counter[:, None] * counter[None, :] % SG
    phase_angle = polarity * 2.0 * math.pi / SG * product.astype(jnp.float32)
    return (jnp.cos(phase_angle), jnp.sin(phase_angle))


def pixel_terms():
    counter = jnp.arange(SG, dtype=jnp.float32)
    pixel_coords = (counter - SG // 2) / SG
    taper_row = 1.0 - 0.8 * ((2.0 * counter + 1.0 - SG) / SG) ** 2
    return (pixel_coords, taper_row[:, None] * taper_row[None, :])


def general_device(
    visibilities, uv_offset, chan_index, counts, row_tile, col_tile, primary_beam, model_image
):
    shards = lax.axis_size("chan")
    owners = lax.axis_size("sub")
    shard_index = lax.axis_index("chan")
    facet_len = primary_beam.shape[1]
    row_dev = facet_len // owners
    band_len = facet_len // shards
    row_tiles = row_dev // SG
    col_tiles = facet_len // SG
    pixel_coords, taper_grid = pixel_terms()
    down_cos, down_sin = centred_table(-1)
    up_cos, up_sin = centred_table(1)
    global_chan = shard_index * CH_DEV + chan_index
    freq_scale = 1.0 + 0.5 * global_chan.astype(jnp.float32) / (shards * CH_DEV)
    u_cells = uv_offset[0] * freq_scale
    v_cells = uv_offset[1] * freq_scale
    row_hot = (row_tile[:, None] == jnp.arange(row_tiles, dtype=jnp.int32)[None, :]).astype(
        jnp.float32
    )
    col_hot = (col_tile[:, None] == jnp.arange(col_tiles, dtype=jnp.int32)[None, :]).astype(
        jnp.float32
    )
    pair_hot = (row_hot[:, :, None] * col_hot[:, None, :]).reshape(SUB_DEV, row_tiles * col_tiles)
    slot_index = jnp.arange(CAP, dtype=jnp.int32)
    live_mask = (slot_index[None, :] < counts).astype(jnp.float32)
    vis_re = visibilities[0] * live_mask
    vis_im = visibilities[1] * live_mask
    a_angle = 2.0 * math.pi * u_cells[:, :, None] * pixel_coords
    b_angle = 2.0 * math.pi * v_cells[:, :, None] * pixel_coords
    terms = (
        live_mask,
        vis_re,
        vis_im,
        jnp.cos(a_angle),
        jnp.sin(a_angle),
        jnp.cos(b_angle),
        jnp.sin(b_angle),
    )
    live_mask, vis_re, vis_im, a_cos, a_sin, b_cos, b_sin = terms
    wb_re = vis_re[:, :, None] * b_cos - vis_im[:, :, None] * b_sin
    wb_im = vis_re[:, :, None] * b_sin + vis_im[:, :, None] * b_cos
    image_re, image_im = complex_einsum("jkq,jkp->jqp", wb_re, wb_im, a_cos, a_sin)
    image_re = image_re * taper_grid
    image_im = image_im * taper_grid
    left_re, left_im = complex_einsum("aq,jqp->jap", down_cos, down_sin, image_re, image_im)
    win_re, win_im = complex_einsum("jap,bp->jab", left_re, left_im, down_cos, down_sin)
    stacked = jnp.concatenate(
        [win_re.reshape(SUB_DEV, SG * SG), win_im.reshape(SUB_DEV, SG * SG)], axis=1
    )
    placed = jnp.dot(pair_hot.T, stacked, precision=precise, preferred_element_type=jnp.float32)
    placed = (
        placed.reshape(row_tiles, col_tiles, 2, SG, SG)
        .transpose(2, 0, 3, 1, 4)
        .reshape(2, row_dev, facet_len)
    )
    band_spec_re, band_spec_im = transform_last(placed[0], placed[1], 1)
    tile_re, tile_im = (
        lax.psum_scatter(band_spec_re, "chan", scatter_dimension=1, tiled=True),
        lax.psum_scatter(band_spec_im, "chan", scatter_dimension=1, tiled=True),
    )
    image_rows_re, image_rows_im = (
        lax.all_to_all(tile_re.T, "sub", split_axis=0, concat_axis=1, tiled=True),
        lax.all_to_all(tile_im.T, "sub", split_axis=0, concat_axis=1, tiled=True),
    )
    sky_re, sky_im = transform_last(image_rows_re, image_rows_im, 1)
    dirty_scale = 1.0 / (SG * SG * math.sqrt(SUB_DEV * owners * CAP * shards))
    dirty_image = sky_re * dirty_scale
    shifted = model_image + primary_beam * dirty_image
    new_model = jnp.sign(shifted) * jnp.maximum(jnp.abs(shifted) - 0.25, 0.0)
    forward_re, forward_im = transform_last(new_model, None, -1)
    back_rows_re, back_rows_im = (
        lax.all_to_all(forward_re, "sub", split_axis=1, concat_axis=0, tiled=True),
        lax.all_to_all(forward_im, "sub", split_axis=1, concat_axis=0, tiled=True),
    )
    grid_band_re = back_rows_re.T
    grid_band_im = back_rows_im.T
    chosen_re = jnp.einsum(
        "jr,ral->jal", row_hot, grid_band_re.reshape(row_tiles, SG, band_len), precision=precise
    )
    chosen_im = jnp.einsum(
        "jr,ral->jal", row_hot, grid_band_im.reshape(row_tiles, SG, band_len), precision=precise
    )
    u_index = col_tile[:, None] * SG + jnp.arange(SG, dtype=jnp.int32)[None, :]
    l_index = shard_index * band_len + jnp.arange(band_len, dtype=jnp.int32)
    product = u_index[:, :, None] * l_index[None, None, :] % facet_len
    phase_angle = -1 * 2.0 * math.pi / facet_len * product.astype(jnp.float32)
    down_col_cos = jnp.cos(phase_angle)
    down_col_sin = jnp.sin(phase_angle)
    part_re, part_im = complex_einsum(
        "jal,jbl->jab", chosen_re, chosen_im, down_col_cos, down_col_sin
    )
    summed_re, summed_im = lax.psum((part_re, part_im), "chan")
    back_win_re = summed_re / facet_len
    back_win_im = summed_im / facet_len
    left_re, left_im = complex_einsum("aq,jab->jqb", up_cos, up_sin, back_win_re, back_win_im)
    model_sub_re, model_sub_im = complex_einsum("jqb,bp->jqp", left_re, left_im, up_cos, up_sin)
    model_sub_re = model_sub_re * taper_grid / SG
    model_sub_im = model_sub_im * taper_grid / SG
    live_mask, vis_re, vis_im, a_cos, a_sin, b_cos, b_sin = terms
    inner_re, inner_im = complex_einsum("jkp,jqp->jkq", a_cos, -a_sin, model_sub_re, model_sub_im)
    pred_re = jnp.sum(b_cos * inner_re + b_sin * inner_im, axis=2)
    pred_im = jnp.sum(b_cos * inner_im - b_sin * inner_re, axis=2)
    factor = 4.0 / SG * live_mask
    pred_re, pred_im = (pred_re * factor, pred_im * factor)
    return (new_model, jnp.stack([pred_re, pred_im]))


def _fit():
    nodes = 0.5 * np.cos(np.pi * (np.arange(400) + 0.5) / 400)
    square = nodes * nodes
    powers = np.vander(square, 9, increasing=True)
    cos_fit = np.linalg.lstsq(powers, np.cos(2 * np.pi * nodes), rcond=None)[0]
    ratio = np.where(nodes == 0, 2 * np.pi, np.sin(2 * np.pi * nodes) / nodes)
    sin_fit = np.linalg.lstsq(powers, ratio, rcond=None)[0]
    return [float(x) for x in cos_fit], [float(x) for x in sin_fit]


COS_FIT, SIN_FIT = _fit()


def cis(turns):
    rest = turns - jnp.round(turns)
    square = rest * rest
    cos = jnp.full_like(rest, COS_FIT[-1])
    sin = jnp.full_like(rest, SIN_FIT[-1])
    for c, s in zip(COS_FIT[-2::-1], SIN_FIT[-2::-1], strict=True):
        cos = cos * square + c
        sin = sin * square + s
    return cos, sin * rest


def halves(x):
    high = x.astype(jnp.bfloat16)
    return high, (x - high.astype(jnp.float32)).astype(jnp.bfloat16)


NN = (((1,), (0,)), ((), ()))
NT = (((1,), (1,)), ((), ()))


def dot3(left, right, dims):
    dot = functools.partial(
        lax.dot_general, dimension_numbers=dims, preferred_element_type=jnp.float32
    )
    return dot(left[0], right[0]) + (dot(left[1], right[0]) + dot(left[0], right[1]))


def window_table():
    a = np.concatenate([np.arange(0, SG, 2), np.arange(1, SG, 2)]) - SG // 2
    q = np.arange(SG) - SG // 2
    taper = 1.0 - 0.8 * ((2.0 * np.arange(SG) + 1.0 - SG) / SG) ** 2
    value = np.exp(-2j * np.pi * np.outer(a, q) / SG) * taper[None, :]
    return np.block([[value.real, -value.imag], [value.imag, value.real]]).astype(np.float32)


def column_table(facet_len, rows):
    p = np.arange(SG) - SG // 2
    b = np.arange(SG)
    taper = 1.0 - 0.8 * ((2.0 * np.arange(SG) + 1.0 - SG) / SG) ** 2
    window = np.exp(-2j * np.pi * np.outer(b - SG // 2, p) / SG) * taper[None, :]
    value = np.exp(2j * np.pi * np.outer(np.arange(facet_len), b) / facet_len) @ window
    value = value.reshape(facet_len // rows, rows, SG)
    top = np.concatenate([value.real, -value.imag], axis=2)
    low = np.concatenate([value.imag, value.real], axis=2)
    return np.concatenate([top, low], axis=1).astype(np.float32)


def phasor_rows(row):
    steps = lax.broadcasted_iota(jnp.int32, (8, CAP), 0).astype(jnp.float32) / SG
    cos, sin = cis(row * steps)
    return cos, sin


def grid_kernel(
    row_ref, col_ref, vis_ref, uv_ref, chan_ref, counts_ref, window_ref, out_ref, a_ref, b_ref,
    *, shards, row_tiles
):
    shard = lax.axis_index("chan")
    owner = lax.axis_index("sub")
    chan = (shard * CH_DEV + chan_ref[...]).astype(jnp.float32)
    scale = 1.0 + 0.5 * chan / (shards * CH_DEV)
    slot = lax.broadcasted_iota(jnp.int32, (SUB_DEV, CAP), 1)
    live = (slot < counts_ref[...]).astype(jnp.float32)
    vis_re = vis_ref[0] * live
    vis_im = vis_ref[1] * live
    window = halves(window_ref[...])
    steps = lax.broadcasted_iota(jnp.int32, (8, CAP), 0).astype(jnp.float32) / SG
    far = []
    for axis in range(2):
        cells = uv_ref[axis] * scale
        far.append((cells, cis(cells * 0.25), cis(cells * 0.5)))

    def phasors(axis, j):
        cells, (c8, s8), (c16, s16) = far[axis]
        cos, sin = cis(cells[j : j + 1] * steps)
        c8, s8, c16, s16 = (x[j : j + 1] for x in (c8, s8, c16, s16))
        re = [cos * c16 + sin * s16, cos * c8 + sin * s8, cos, cos * c8 - sin * s8]
        im = [sin * c16 - cos * s16, sin * c8 - cos * s8, sin, sin * c8 + cos * s8]
        return jnp.concatenate(re, axis=0), jnp.concatenate(im, axis=0)

    for j in range(SUB_DEV):
        a_re, a_im = phasors(0, j)
        a_ref[j] = jnp.concatenate([a_re, a_im], axis=0)
        b_re, b_im = phasors(1, j)
        hat = dot3(window, halves(jnp.concatenate([b_re, b_im], axis=0)), NN)
        b_ref[j] = hat
        hat_re, hat_im = hat[:SG], hat[SG:]
        re, im = vis_re[j : j + 1], vis_im[j : j + 1]
        left = jnp.concatenate([re * hat_re - im * hat_im, re * hat_im + im * hat_re], axis=1)
        right = jnp.concatenate(
            [jnp.concatenate([a_re, -a_im], axis=1), jnp.concatenate([a_im, a_re], axis=1)], axis=0
        )
        image = dot3(halves(left), halves(right), NT)
        out_ref[0:RADIX, j, :] = jnp.concatenate([image[:RADIX], image[RADIX:]], axis=1)
    line = lax.broadcasted_iota(jnp.int32, (SUB_DEV, LANES), 0)
    lane = lax.broadcasted_iota(jnp.int32, (SUB_DEV, LANES), 1)
    info = jnp.zeros((SUB_DEV, LANES), jnp.int32)
    for j in range(SUB_DEV):
        info = jnp.where((line == j) & (lane == 0), owner * row_tiles + row_ref[j], info)
        info = jnp.where((line == j) & (lane == 1), col_ref[j], info)
    out_ref[RADIX] = info.astype(jnp.float32)


def real_from_half(h0, h8, hr, hi):
    c1, c3, r = math.cos(math.pi / 8), math.cos(3 * math.pi / 8), math.sqrt(0.5)
    (r1, r2, r3, r4, r5, r6, r7), (i1, i2, i3, i4, i5, i6, i7) = hr, hi
    p, q, s, d = h0 + h8, h0 - h8, r2 + r6, r * (r2 - r6)
    t = p + r4
    even = [t + s, q + d, p - r4, q - d, t - s]
    s17, d17, s35, d35 = r1 + r7, r1 - r7, r3 + r5, r3 - r5
    odd = [s17 + s35, c1 * d17 + c3 * d35, r * (s17 - s35), c3 * d17 - c1 * d35]
    cos = [even[m] + odd[m] for m in range(4)] + [even[4]] + [even[m] - odd[m] for m in (3, 2, 1, 0)]
    s17, d17, s35, d35 = i1 + i7, i1 - i7, i3 + i5, i3 - i5
    odd = [None, c3 * s17 + c1 * s35, r * (d17 + d35), c1 * s17 - c3 * s35, d17 - d35]
    s26 = r * (i2 + i6)
    even = [None, s26 + i4, i2 - i6, s26 - i4]
    sin = [None] + [odd[m] + even[m] for m in (1, 2, 3)] + [odd[4]] + [odd[m] - even[m] for m in (3, 2, 1)]
    out = [cos[0]] + [cos[m] - sin[m] for m in range(1, 8)] + [cos[8]]
    return out + [cos[m] + sin[m] for m in range(7, 0, -1)]


def half_from_real(x):
    c1, c3, r = math.cos(math.pi / 8), math.cos(3 * math.pi / 8), math.sqrt(0.5)
    s = [None] + [x[m] + x[16 - m] for m in range(1, 8)]
    d = [None] + [x[m] - x[16 - m] for m in range(1, 8)]
    p, q = x[0] + x[8], x[0] - x[8]
    s17, d17, s35, d35, s26, d26 = s[1] + s[7], s[1] - s[7], s[3] + s[5], s[3] - s[5], s[2] + s[6], r * (s[2] - s[6])
    t = p + s[4]
    even = [t + s26, q + d26, p - s[4], q - d26, t - s26]
    odd = [s17 + s35, c1 * d17 + c3 * d35, r * (s17 - s35), c3 * d17 - c1 * d35]
    re = [even[m] + odd[m] for m in range(4)] + [even[4]] + [even[m] - odd[m] for m in (3, 2, 1, 0)]
    s17, d17, s35, d35 = d[1] + d[7], d[1] - d[7], d[3] + d[5], d[3] - d[5]
    odd = [None, c3 * s17 + c1 * s35, r * (d17 + d35), c1 * s17 - c3 * s35, d17 - d35]
    s26 = r * (d[2] + d[6])
    even = [None, s26 + d[4], d[2] - d[6], s26 - d[4]]
    im = [None] + [odd[m] + even[m] for m in (1, 2, 3)] + [odd[4]] + [odd[m] - even[m] for m in (3, 2, 1)] + [None]
    return re, im


def image_kernel(
    own_ref, pair_ref, table_ref, beam_ref, model_ref, new_ref, own_out, pair_out,
    wide_ref, spec_ref, back_ref, *, shards, scale
):
    own_blocks = own_ref.shape[0]
    blocks = [own_ref.at[t] for t in range(own_blocks)] + [pair_ref.at[t] for t in range(own_blocks)]
    rows = beam_ref.shape[0]
    info = jnp.concatenate([b[RADIX] for b in blocks], axis=0) * (1.0 / shards)
    info = jnp.concatenate([info, info], axis=0)
    line = lax.broadcasted_iota(jnp.int32, (LANES, LANES), 0)
    lane = lax.broadcasted_iota(jnp.int32, (LANES, LANES), 1)
    upper = (line >= LANES // 2).astype(jnp.float32)
    fine = 2.0 * info[:, 0:1] + upper
    cos, sin = cis(fine * lane.astype(jnp.float32) * (1.0 / LANES))
    mix = jnp.concatenate(
        [jnp.concatenate([cos, sin], axis=1), jnp.concatenate([-sin, cos], axis=1)], axis=0
    )
    mix = halves(mix)
    column = jnp.broadcast_to(info[:, 1:2], (LANES, LANES)).T[:rows]
    phase_cos, phase_sin = cis(column * line[:rows].astype(jnp.float32) * (1.0 / 64))
    table = jnp.concatenate([table_ref[...], table_ref[...]], axis=1)
    table = jnp.concatenate(
        [jnp.where(lane < LANES // 2, table, 0.0), jnp.where(lane < LANES // 2, 0.0, table)], axis=0
    )
    down = halves(table)
    up = halves(table.T)
    for k in range(RADIX // 2):
        stack = [b[k] for b in blocks] + [b[RADIX // 2 + k] for b in blocks]
        wide = dot3(down, halves(jnp.concatenate(stack, axis=0)), NT)
        for b in range(2):
            re = wide[2 * b * rows : (2 * b + 1) * rows]
            im = wide[(2 * b + 1) * rows : (2 * b + 2) * rows]
            both = jnp.concatenate(
                [re * phase_cos - im * phase_sin, re * phase_sin + im * phase_cos], axis=1
            )
            high, low = halves(both)
            at = pl.ds((2 * k + b) * rows, rows)
            wide_ref[0, at] = high
            wide_ref[1, at] = low
    group = 4 * rows
    for g in range(RADIX // 4):
        at = pl.ds(g * group, group)
        spec_ref[at] = dot3((wide_ref[0, at], wide_ref[1, at]), mix, NN)
    twist = [cis(lax.broadcasted_iota(jnp.int32, (8, LANES), 1).astype(jnp.float32) * (a / (RADIX * LANES))) for a in range(1, RADIX)]

    for tile in range(rows // 8):
        at = lambda a: pl.ds(a * rows + tile * 8, 8)
        re = [spec_ref[at(0), :LANES]]
        im = [None]
        for a in range(1, RADIX):
            x, y = spec_ref[at(a), :LANES], spec_ref[at(a), LANES:]
            c, s = twist[a - 1]
            re.append(x * c - y * s)
            im.append(x * s + y * c)
        hr = [re[a] + re[RADIX - a] for a in range(1, 8)]
        hi = [im[a] - im[RADIX - a] for a in range(1, 8)]
        dirty = real_from_half(re[0], re[8], hr, hi)
        new = []
        for m in range(RADIX):
            where = (slice(tile * 8, tile * 8 + 8), slice(m * LANES, (m + 1) * LANES))
            shifted = model_ref[where] + beam_ref[where] * (dirty[m] * scale)
            value = shifted - jnp.clip(shifted, -0.25, 0.25)
            new_ref[where] = value
            new.append(value)
        re, im = half_from_real(new)
        back_ref[at(0), :LANES] = re[0]
        back_ref[at(0), LANES:] = jnp.zeros_like(re[0])
        for a in range(1, RADIX):
            c, s = twist[a - 1]
            if a == 8:
                back_ref[at(a), :LANES] = re[8] * c
                back_ref[at(a), LANES:] = -(re[8] * s)
                continue
            x, y = (re[a], im[a]) if a < 8 else (re[RADIX - a], -im[RADIX - a])
            back_ref[at(a), :LANES] = x * c - y * s
            back_ref[at(a), LANES:] = -(x * s + y * c)
    for g in range(RADIX // 4):
        at = pl.ds(g * group, group)
        spec_ref[at] = dot3(halves(back_ref[at]), mix, NT)
    for k in range(RADIX // 2):
        stack = []
        for b in range(2):
            at = pl.ds((2 * k + b) * rows, rows)
            re, im = spec_ref[at, :LANES], spec_ref[at, LANES:]
            stack.append(re * phase_cos + im * phase_sin)
            stack.append(im * phase_cos - re * phase_sin)
        part = dot3(up, halves(jnp.concatenate(stack, axis=0)), NN).T
        for h in range(2):
            for t in range(own_blocks):
                first = h * LANES // 2 + t * SUB_DEV
                own_out[t, h * RADIX // 2 + k] = part[first : first + SUB_DEV]
                first += own_blocks * SUB_DEV
                pair_out[t, h * RADIX // 2 + k] = part[first : first + SUB_DEV]


def predict_kernel(x0, x1, x2, x3, a_ref, b_ref, counts_ref, out_ref, *, scale):
    total = (x0[...] + x1[...]) + (x2[...] + x3[...])
    slot = lax.broadcasted_iota(jnp.int32, (1, CAP), 1)
    for j in range(SUB_DEV):
        rows = total[:, j, :]
        left = halves(jnp.concatenate([rows[:, : LANES // 2], rows[:, LANES // 2 :]], axis=0))
        a_re, a_im = a_ref[j, :SG], a_ref[j, SG:]
        inner_re = dot3(left, halves(jnp.concatenate([a_re, a_im], axis=0)), NN)
        inner_im = dot3(left, halves(jnp.concatenate([-a_im, a_re], axis=0)), NN)
        b_re, b_im = b_ref[j, :SG], b_ref[j, SG:]
        factor = jnp.where(slot < counts_ref[j : j + 1], scale, 0.0)
        re = jnp.sum(b_re * inner_re + b_im * inner_im, axis=0, keepdims=True)
        im = jnp.sum(b_re * inner_im - b_im * inner_re, axis=0, keepdims=True)
        out_ref[0, j : j + 1] = re * factor
        out_ref[1, j : j + 1] = im * factor


def swap(x, axis, mask):
    size = lax.axis_size(axis)
    return lax.ppermute(x, axis, [(i, i ^ mask) for i in range(size)])


def fast_device(
    visibilities, uv_offset, chan_index, counts, row_tile, col_tile, primary_beam, model_image
):
    shards = lax.axis_size("chan")
    owners = lax.axis_size("sub")
    rows, facet_len = primary_beam.shape
    f32 = jnp.float32
    vmem = pl.BlockSpec(memory_space=pltpu.VMEM)
    smem = pl.BlockSpec(memory_space=pltpu.SMEM)
    shape = jax.ShapeDtypeStruct
    payload, a_rows, b_rows = pl.pallas_call(
        functools.partial(grid_kernel, shards=shards, row_tiles=facet_len // owners // SG),
        out_shape=(
            shape((RADIX + 1, SUB_DEV, LANES), f32),
            shape((SUB_DEV, 2 * SG, CAP), f32),
            shape((SUB_DEV, 2 * SG, CAP), f32),
        ),
        in_specs=[smem, smem] + [vmem] * 5,
        out_specs=[vmem] * 3,
        name="grid",
    )(row_tile, col_tile, visibilities, uv_offset, chan_index, counts, window_table())
    block = lax.axis_index("chan") * owners + lax.axis_index("sub")
    table = lax.dynamic_index_in_dim(jnp.asarray(column_table(facet_len, rows)), block, 0, False)
    payload = payload + sum(swap(payload, "chan", k) for k in range(1, shards))
    own = jnp.stack([payload] + [swap(payload, "sub", k) for k in range(2, owners, 2)])
    pair = swap(own, "sub", 1)
    part = shape((owners // 2, RADIX, SUB_DEV, LANES), f32)
    new_model, own, pair = pl.pallas_call(
        functools.partial(
            image_kernel,
            shards=shards,
            scale=1.0 / (SG * SG * math.sqrt(SUB_DEV * owners * CAP * shards)),
        ),
        out_shape=(shape((rows, facet_len), f32), part, part),
        in_specs=[vmem] * 5,
        out_specs=[vmem] * 3,
        scratch_shapes=[
            pltpu.VMEM((2, RADIX * rows, 2 * LANES), jnp.bfloat16),
            pltpu.VMEM((RADIX * rows, 2 * LANES), f32),
            pltpu.VMEM((RADIX * rows, 2 * LANES), f32),
        ],
        name="image",
    )(own, pair, table, primary_beam, model_image)
    own = own + swap(pair, "sub", 1)
    part = own[0] + sum(swap(own[k // 2], "sub", k) for k in range(2, owners, 2))
    parts = [part] + [swap(part, "chan", k) for k in range(1, shards)]
    predicted = pl.pallas_call(
        functools.partial(predict_kernel, scale=4.0 / SG / SG / facet_len),
        out_shape=shape((2, SUB_DEV, CAP), f32),
        in_specs=[vmem] * 7,
        out_specs=vmem,
        name="predict",
    )(*parts, a_rows, b_rows, counts)
    return new_model, predicted


def on_device(*arrays):
    shards, owners = lax.axis_size("chan"), lax.axis_size("sub")
    rows, facet_len = arrays[6].shape
    fits = (
        shards == 4
        and owners == 8
        and 2 * rows == LANES
        and facet_len == RADIX * LANES
        and 2 * owners * SUB_DEV == LANES
    )
    return (fast_device if fits else general_device)(*arrays)


def solution(mesh):
    in_specs = (
        P(None, "sub", "chan"),
        P(None, "sub", "chan"),
        P("sub", "chan"),
        P("sub", "chan"),
        P("sub"),
        P("sub"),
        P(("chan", "sub"), None),
        P(("chan", "sub"), None),
    )
    out_specs = (P(("chan", "sub"), None), P(None, "sub", "chan"))
    return jax.shard_map(
        on_device, mesh=mesh, in_specs=in_specs, out_specs=out_specs, check_vma=False
    )
```

profile of v0, /device:TPU:0, one launch (start us, length us, event | category | flops | bytes accessed | tf_op | source)
XLA Modules:
  0.0 52.8 jit_solution(4270635360302704154)
XLA Ops:
  0.6 1.3 %copy.12.counts_ref = s32[8,1]{1,0:T(8,128)} copy(s32[8,1]{0,1:T(1,128)} %param.13) | data formatting | bytes 64 | tf_op args[3]
  2.0 2.9 %grid.1 = (f32[17,8,128]{2,1,0:T(8,128)}, f32[8,64,256]{2,1,0:T(8,128)}, f32[8,64,256]{2,1,0:T(8,128)}) custom-call(s32[8]{0:T(128)} %row_ref.1, s32[8]{0:T(128)} %col_ref.1, f32[2,8,256]{2,1,0:T(8,128)} %vis_ref.1, f32[2,8,256]{2,1,0:T(8,128)} %uv_ref.1, s32[8,256]{1,0:T(8,128)} %chan_ref.1, s32[8,1]{1,0:T(8,128)} %copy.12.counts_ref, ...), custom_call_target="tpu_custom_call" | custom-call | tf_op jit(solution)/shard_map/grid/pallas_call | solution.py:477
  4.8 5.1 %collective-permute-start.2 = (f32[17,8,128]{2,1,0:T(8,128)}, f32[17,8,128]{2,1,0:T(8,128)S(1)}, u32[]{:S(2)}, u32[]{:S(2)}) collective-permute-start(f32[17,8,128]{2,1,0:T(8,128)} %get-tuple-element.8), channel_id=1, source_target_pairs={{0,24},{8,16},{16,8},{24,0},{1,25},{9,17},{17,9},{25,1},{2,26},{10... | collective-permute-start | bytes 208904 | tf_op jit(solution)/shard_map/ppermute | solution.py:464
  9.9 0.6 %collective-permute-start = (f32[17,8,128]{2,1,0:T(8,128)}, f32[17,8,128]{2,1,0:T(8,128)S(1)}, u32[]{:S(2)}, u32[]{:S(2)}) collective-permute-start(f32[17,8,128]{2,1,0:T(8,128)} %get-tuple-element.8), channel_id=1, source_target_pairs={{0,8},{8,0},{16,24},{24,16},{1,9},{9,1},{17,25},{25,17},{2,10},{10... | collective-permute-start | bytes 208904 | tf_op jit(solution)/shard_map/ppermute | solution.py:464
  10.5 2.3 %collective-permute-done.2 = f32[17,8,128]{2,1,0:T(8,128)S(1)} collective-permute-done((f32[17,8,128]{2,1,0:T(8,128)}, f32[17,8,128]{2,1,0:T(8,128)S(1)}, u32[]{:S(2)}, u32[]{:S(2)}) %collective-permute-start.2) | collective-permute-done | bytes 69664 | tf_op jit(solution)/shard_map/ppermute | solution.py:464
  12.8 3.2 %collective-permute-done.1 = f32[17,8,128]{2,1,0:T(8,128)S(1)} collective-permute-done((f32[17,8,128]{2,1,0:T(8,128)}, f32[17,8,128]{2,1,0:T(8,128)S(1)}, u32[]{:S(2)}, u32[]{:S(2)}) %collective-permute-start.1) | collective-permute-done | bytes 69664 | tf_op jit(solution)/shard_map/ppermute | solution.py:464
  16.0 0.9 %add_add_fusion = f32[17,8,128]{2,1,0:T(8,128)S(1)} fusion(f32[17,8,128]{2,1,0:T(8,128)} %get-tuple-element.8, f32[17,8,128]{2,1,0:T(8,128)S(1)} %collective-permute-done.2, f32[17,8,128]{2,1,0:T(8,128)S(1)} %collective-permute-done, f32[17,8,128]{2,1,0:T(8,128)S(1)} %collective-permute-done.1), kind=kLoop, calls=%fused_computation.1 | loop fusion | flops 52224 | bytes 348160 | tf_op jit(solution)/shard_map/add | solution.py:490
  16.9 2.5 %collective-permute-start.5 = (f32[17,8,128]{2,1,0:T(8,128)S(1)}, f32[17,8,128]{2,1,0:T(8,128)S(1)}, u32[]{:S(2)}, u32[]{:S(2)}) collective-permute-start(f32[17,8,128]{2,1,0:T(8,128)S(1)} %add_add_fusion), channel_id=1, source_target_pairs={{0,6},{1,7},{2,4},{3,5},{4,2},{5,3},{6,0},{7,1},{8,14},{9,15},{10,... | collective-permute-start | bytes 208904 | tf_op jit(solution)/shard_map/ppermute | solution.py:464
  19.5 0.5 collective-permute-start.4
  20.0 0.5 %collective-permute-start.3 = (f32[17,8,128]{2,1,0:T(8,128)S(1)}, f32[17,8,128]{2,1,0:T(8,128)S(1)}, u32[]{:S(2)}, u32[]{:S(2)}) collective-permute-start(f32[17,8,128]{2,1,0:T(8,128)S(1)} %add_add_fusion), channel_id=1, source_target_pairs={{0,2},{1,3},{2,0},{3,1},{4,6},{5,7},{6,4},{7,5},{8,10},{9,11},{10,... | collective-permute-start | bytes 208904 | tf_op jit(solution)/shard_map/ppermute | solution.py:464
  20.5 1.8 %collective-permute-done.5 = f32[17,8,128]{2,1,0:T(8,128)S(1)} collective-permute-done((f32[17,8,128]{2,1,0:T(8,128)S(1)}, f32[17,8,128]{2,1,0:T(8,128)S(1)}, u32[]{:S(2)}, u32[]{:S(2)}) %collective-permute-start.5) | collective-permute-done | bytes 69664 | tf_op jit(solution)/shard_map/ppermute | solution.py:464
  22.3 1.4 %collective-permute-done.4 = f32[17,8,128]{2,1,0:T(8,128)S(1)} collective-permute-done((f32[17,8,128]{2,1,0:T(8,128)S(1)}, f32[17,8,128]{2,1,0:T(8,128)S(1)}, u32[]{:S(2)}, u32[]{:S(2)}) %collective-permute-start.4) | collective-permute-done | bytes 69664 | tf_op jit(solution)/shard_map/ppermute | solution.py:464
  23.8 0.5 collective-permute-done.3
  24.3 0.1 collective-permute-start.6
  24.4 1.5 %dynamic-slice_bitcast_fusion.table_ref = f32[128,64]{1,0:T(8,128)} fusion(f32[32,128,64]{2,1,0:T(8,128)} %constant.21.clone, s32[]{:T(128)S(6)} %select_n.4), kind=kLoop, calls=%fused_computation.7 | loop fusion | bytes 65540 | tf_op jit(solution)/shard_map/jit(dynamic_index_in_dim)/squeeze | solution.py:489
  25.9 0.0 collective-permute-done.6.pair_ref
  25.9 0.7 %copy-done.1 = f32[4,17,8,128]{3,2,1,0:T(8,128)} copy-done((f32[4,17,8,128]{3,2,1,0:T(8,128)}, f32[4,17,8,128]{3,2,1,0:T(8,128)S(1)}, u32[]{:S(2)}) %copy-start.1) | copy-done | bytes 278552
  26.6 4.7 %image.1 = (f32[64,2048]{1,0:T(8,128)}, f32[4,16,8,128]{3,2,1,0:T(8,128)}, f32[4,16,8,128]{3,2,1,0:T(8,128)}) custom-call(f32[4,17,8,128]{3,2,1,0:T(8,128)} %copy-done, f32[4,17,8,128]{3,2,1,0:T(8,128)} %copy-done.1, f32[128,64]{1,0:T(8,128)} %dynamic-slice_bitcast_fusion.table_ref, f32[64,2048]{1,0:T(8,128)} %beam_ref.1, f32[64,2048]{1,0:T(8,128)} %model_ref.1), custom_call_target="tpu_custom_call" | custom-call | tf_op jit(solution)/shard_map/image/pallas_call | solution.py:494
  31.3 0.4 collective-permute-start.7
  31.7 1.4 %collective-permute-done.7 = f32[4,16,8,128]{3,2,1,0:T(8,128)S(1)} collective-permute-done((f32[4,16,8,128]{3,2,1,0:T(8,128)}, f32[4,16,8,128]{3,2,1,0:T(8,128)S(1)}, u32[]{:S(2)}, u32[]{:S(2)}) %collective-permute-start.7) | collective-permute-done | bytes 262176 | tf_op jit(solution)/shard_map/ppermute | solution.py:464
  33.1 1.0 %add.33 = f32[4,16,8,128]{3,2,1,0:T(8,128)S(1)} add(f32[4,16,8,128]{3,2,1,0:T(8,128)} %get-tuple-element.10, f32[4,16,8,128]{3,2,1,0:T(8,128)S(1)} %collective-permute-done.7) | non-fusion elementwise | flops 65536 | bytes 786432 | tf_op jit(solution)/shard_map/add | solution.py:510
  34.1 1.6 %collective-permute-start.9 = (f32[16,8,128]{2,1,0:T(8,128)S(1)}, f32[16,8,128]{2,1,0:T(8,128)S(1)}, u32[]{:S(2)}, u32[]{:S(2)}) collective-permute-start(f32[16,8,128]{2,1,0:T(8,128)S(1)} %get-tuple-element.14), channel_id=1, source_target_pairs={{0,4},{1,5},{2,6},{3,7},{4,0},{5,1},{6,2},{7,3},{8,12},{9,13},{10,... | collective-permute-start | bytes 196616 | tf_op jit(solution)/shard_map/ppermute | solution.py:464
  35.7 0.5 collective-permute-start.10
  36.2 1.5 %collective-permute-start.8 = (f32[16,8,128]{2,1,0:T(8,128)S(1)}, f32[16,8,128]{2,1,0:T(8,128)S(1)}, u32[]{:S(2)}, u32[]{:S(2)}) collective-permute-start(f32[16,8,128]{2,1,0:T(8,128)S(1)} %get-tuple-element.16), channel_id=1, source_target_pairs={{0,2},{1,3},{2,0},{3,1},{4,6},{5,7},{6,4},{7,5},{8,10},{9,11},{10,... | collective-permute-start | bytes 196616 | tf_op jit(solution)/shard_map/ppermute | solution.py:464
  37.7 0.9 %collective-permute-done.9 = f32[16,8,128]{2,1,0:T(8,128)S(1)} collective-permute-done((f32[16,8,128]{2,1,0:T(8,128)S(1)}, f32[16,8,128]{2,1,0:T(8,128)S(1)}, u32[]{:S(2)}, u32[]{:S(2)}) %collective-permute-start.9) | collective-permute-done | bytes 65568 | tf_op jit(solution)/shard_map/ppermute | solution.py:464
  38.5 2.8 %collective-permute-done.10 = f32[16,8,128]{2,1,0:T(8,128)S(1)} collective-permute-done((f32[16,8,128]{2,1,0:T(8,128)S(1)}, f32[16,8,128]{2,1,0:T(8,128)S(1)}, u32[]{:S(2)}, u32[]{:S(2)}) %collective-permute-start.10) | collective-permute-done | bytes 65568 | tf_op jit(solution)/shard_map/ppermute | solution.py:464
  41.4 2.7 %collective-permute-start.13 = (f32[16,8,128]{2,1,0:T(8,128)S(1)}, f32[16,8,128]{2,1,0:T(8,128)S(1)}, u32[]{:S(2)}, u32[]{:S(2)}) collective-permute-start(f32[16,8,128]{2,1,0:T(8,128)S(1)} %fusion.x0), channel_id=1, source_target_pairs={{0,24},{8,16},{16,8},{24,0},{1,25},{9,17},{17,9},{25,1},{2,26},{10... | collective-permute-start | bytes 196616 | tf_op jit(solution)/shard_map/ppermute | solution.py:464
  44.1 1.7 %collective-permute-start.11 = (f32[16,8,128]{2,1,0:T(8,128)S(1)}, f32[16,8,128]{2,1,0:T(8,128)S(1)}, u32[]{:S(2)}, u32[]{:S(2)}) collective-permute-start(f32[16,8,128]{2,1,0:T(8,128)S(1)} %fusion.x0), channel_id=1, source_target_pairs={{0,8},{8,0},{16,24},{24,16},{1,9},{9,1},{17,25},{25,17},{2,10},{10... | collective-permute-start | bytes 196616 | tf_op jit(solution)/shard_map/ppermute | solution.py:464
  45.9 1.8 %collective-permute-done.13.x3 = f32[16,8,128]{2,1,0:T(8,128)S(1)} collective-permute-done((f32[16,8,128]{2,1,0:T(8,128)S(1)}, f32[16,8,128]{2,1,0:T(8,128)S(1)}, u32[]{:S(2)}, u32[]{:S(2)}) %collective-permute-start.13) | collective-permute-done | bytes 65568 | tf_op jit(solution)/shard_map/ppermute | solution.py:464
  47.6 2.1 %collective-permute-done.12.x2 = f32[16,8,128]{2,1,0:T(8,128)S(1)} collective-permute-done((f32[16,8,128]{2,1,0:T(8,128)S(1)}, f32[16,8,128]{2,1,0:T(8,128)S(1)}, u32[]{:S(2)}, u32[]{:S(2)}) %collective-permute-start.12) | collective-permute-done | bytes 65568 | tf_op jit(solution)/shard_map/ppermute | solution.py:464
  49.8 0.6 %copy-done.4 = f32[16,8,128]{2,1,0:T(8,128)} copy-done((f32[16,8,128]{2,1,0:T(8,128)}, f32[16,8,128]{2,1,0:T(8,128)S(1)}, u32[]{:S(2)}) %copy-start.4) | copy-done | bytes 65560
  50.4 2.4 %predict.1 = f32[2,8,256]{2,1,0:T(8,128)} custom-call(f32[16,8,128]{2,1,0:T(8,128)} %copy-done.2, f32[16,8,128]{2,1,0:T(8,128)} %copy-done.5, f32[16,8,128]{2,1,0:T(8,128)} %copy-done.4, f32[16,8,128]{2,1,0:T(8,128)} %copy-done.3, f32[8,64,256]{2,1,0:T(8,128)} %get-tuple-element.12.a_ref, f32[8,64,256]{2,1,0:T(8,128)} %get-tuple-element.13.b_ref, ...), custom_call_target="tpu_custom_call" | custom-call | tf_op jit(solution)/shard_map/predict/pallas_call | solution.py:513
  (18 shorter events, 0.1 us)
Async XLA Ops:
  4.8 8.0 %collective-permute-start.2 = (f32[17,8,128]{2,1,0:T(8,128)}, f32[17,8,128]{2,1,0:T(8,128)S(1)}, u32[]{:S(2)}, u32[]{:S(2)}) collective-permute-start(f32[17,8,128]{2,1,0:T(8,128)} %get-tuple-element.8), channel_id=1, source_target_pairs={{0,24},{8,16},{16,8},{24,0},{1,25},{9,17},{17,9},{25,1},{2,26},{10... | collective-permute-start | bytes 208904 | tf_op jit(solution)/shard_map/ppermute | solution.py:464
  9.9 6.1 %collective-permute-start.1 = (f32[17,8,128]{2,1,0:T(8,128)}, f32[17,8,128]{2,1,0:T(8,128)S(1)}, u32[]{:S(2)}, u32[]{:S(2)}) collective-permute-start(f32[17,8,128]{2,1,0:T(8,128)} %get-tuple-element.8), channel_id=1, source_target_pairs={{0,16},{8,24},{16,0},{24,8},{1,17},{9,25},{17,1},{25,9},{2,18},{10... | collective-permute-start | bytes 208904 | tf_op jit(solution)/shard_map/ppermute | solution.py:464
  9.9 6.1 %collective-permute-start = (f32[17,8,128]{2,1,0:T(8,128)}, f32[17,8,128]{2,1,0:T(8,128)S(1)}, u32[]{:S(2)}, u32[]{:S(2)}) collective-permute-start(f32[17,8,128]{2,1,0:T(8,128)} %get-tuple-element.8), channel_id=1, source_target_pairs={{0,8},{8,0},{16,24},{24,16},{1,9},{9,1},{17,25},{25,17},{2,10},{10... | collective-permute-start | bytes 208904 | tf_op jit(solution)/shard_map/ppermute | solution.py:464
  16.9 5.4 %collective-permute-start.5 = (f32[17,8,128]{2,1,0:T(8,128)S(1)}, f32[17,8,128]{2,1,0:T(8,128)S(1)}, u32[]{:S(2)}, u32[]{:S(2)}) collective-permute-start(f32[17,8,128]{2,1,0:T(8,128)S(1)} %add_add_fusion), channel_id=1, source_target_pairs={{0,6},{1,7},{2,4},{3,5},{4,2},{5,3},{6,0},{7,1},{8,14},{9,15},{10,... | collective-permute-start | bytes 208904 | tf_op jit(solution)/shard_map/ppermute | solution.py:464
  19.5 4.3 %collective-permute-start.4 = (f32[17,8,128]{2,1,0:T(8,128)S(1)}, f32[17,8,128]{2,1,0:T(8,128)S(1)}, u32[]{:S(2)}, u32[]{:S(2)}) collective-permute-start(f32[17,8,128]{2,1,0:T(8,128)S(1)} %add_add_fusion), channel_id=1, source_target_pairs={{0,4},{1,5},{2,6},{3,7},{4,0},{5,1},{6,2},{7,3},{8,12},{9,13},{10,... | collective-permute-start | bytes 208904 | tf_op jit(solution)/shard_map/ppermute | solution.py:464
  20.0 4.3 %collective-permute-start.3 = (f32[17,8,128]{2,1,0:T(8,128)S(1)}, f32[17,8,128]{2,1,0:T(8,128)S(1)}, u32[]{:S(2)}, u32[]{:S(2)}) collective-permute-start(f32[17,8,128]{2,1,0:T(8,128)S(1)} %add_add_fusion), channel_id=1, source_target_pairs={{0,2},{1,3},{2,0},{3,1},{4,6},{5,7},{6,4},{7,5},{8,10},{9,11},{10,... | collective-permute-start | bytes 208904 | tf_op jit(solution)/shard_map/ppermute | solution.py:464
  24.3 1.6 %copy-start = (f32[4,17,8,128]{3,2,1,0:T(8,128)}, f32[4,17,8,128]{3,2,1,0:T(8,128)S(1)}, u32[]{:S(2)}) copy-start(f32[4,17,8,128]{3,2,1,0:T(8,128)S(1)} %pad_maximum_fusion.own_ref) | copy-start | bytes 835588
  24.3 1.6 %collective-permute-start.6 = (f32[4,17,8,128]{3,2,1,0:T(8,128)S(1)}, f32[4,17,8,128]{3,2,1,0:T(8,128)S(1)}, u32[]{:S(2)}, u32[]{:S(2)}) collective-permute-start(f32[4,17,8,128]{3,2,1,0:T(8,128)S(1)} %pad_maximum_fusion.own_ref), channel_id=1, source_target_pairs={{0,1},{1,0},{2,3},{3,2},{4,5},{5,4},{6,7},{7,6},{8,9},{9,8},{10,11... | collective-permute-start | bytes 835592 | tf_op jit(solution)/shard_map/ppermute | solution.py:464
  25.9 0.7 %copy-start.1 = (f32[4,17,8,128]{3,2,1,0:T(8,128)}, f32[4,17,8,128]{3,2,1,0:T(8,128)S(1)}, u32[]{:S(2)}) copy-start(f32[4,17,8,128]{3,2,1,0:T(8,128)S(1)} %collective-permute-done.6.pair_ref) | copy-start | bytes 835588
  31.3 1.8 %collective-permute-start.7 = (f32[4,16,8,128]{3,2,1,0:T(8,128)}, f32[4,16,8,128]{3,2,1,0:T(8,128)S(1)}, u32[]{:S(2)}, u32[]{:S(2)}) collective-permute-start(f32[4,16,8,128]{3,2,1,0:T(8,128)} %get-tuple-element.11), channel_id=1, source_target_pairs={{0,1},{1,0},{2,3},{3,2},{4,5},{5,4},{6,7},{7,6},{8,9},{9,8},{10,11... | collective-permute-start | bytes 786440 | tf_op jit(solution)/shard_map/ppermute | solution.py:464
  34.1 4.4 %collective-permute-start.9 = (f32[16,8,128]{2,1,0:T(8,128)S(1)}, f32[16,8,128]{2,1,0:T(8,128)S(1)}, u32[]{:S(2)}, u32[]{:S(2)}) collective-permute-start(f32[16,8,128]{2,1,0:T(8,128)S(1)} %get-tuple-element.14), channel_id=1, source_target_pairs={{0,4},{1,5},{2,6},{3,7},{4,0},{5,1},{6,2},{7,3},{8,12},{9,13},{10,... | collective-permute-start | bytes 196616 | tf_op jit(solution)/shard_map/ppermute | solution.py:464
  35.7 5.7 %collective-permute-start.10 = (f32[16,8,128]{2,1,0:T(8,128)S(1)}, f32[16,8,128]{2,1,0:T(8,128)S(1)}, u32[]{:S(2)}, u32[]{:S(2)}) collective-permute-start(f32[16,8,128]{2,1,0:T(8,128)S(1)} %get-tuple-element.15), channel_id=1, source_target_pairs={{0,6},{1,7},{2,4},{3,5},{4,2},{5,3},{6,0},{7,1},{8,14},{9,15},{10,... | collective-permute-start | bytes 196616 | tf_op jit(solution)/shard_map/ppermute | solution.py:464
  36.2 5.2 %collective-permute-start.8 = (f32[16,8,128]{2,1,0:T(8,128)S(1)}, f32[16,8,128]{2,1,0:T(8,128)S(1)}, u32[]{:S(2)}, u32[]{:S(2)}) collective-permute-start(f32[16,8,128]{2,1,0:T(8,128)S(1)} %get-tuple-element.16), channel_id=1, source_target_pairs={{0,2},{1,3},{2,0},{3,1},{4,6},{5,7},{6,4},{7,5},{8,10},{9,11},{10,... | collective-permute-start | bytes 196616 | tf_op jit(solution)/shard_map/ppermute | solution.py:464
  41.4 8.4 %copy-start.2 = (f32[16,8,128]{2,1,0:T(8,128)}, f32[16,8,128]{2,1,0:T(8,128)S(1)}, u32[]{:S(2)}) copy-start(f32[16,8,128]{2,1,0:T(8,128)S(1)} %fusion.x0) | copy-start | bytes 196612
  41.4 6.2 %collective-permute-start.13 = (f32[16,8,128]{2,1,0:T(8,128)S(1)}, f32[16,8,128]{2,1,0:T(8,128)S(1)}, u32[]{:S(2)}, u32[]{:S(2)}) collective-permute-start(f32[16,8,128]{2,1,0:T(8,128)S(1)} %fusion.x0), channel_id=1, source_target_pairs={{0,24},{8,16},{16,8},{24,0},{1,25},{9,17},{17,9},{25,1},{2,26},{10... | collective-permute-start | bytes 196616 | tf_op jit(solution)/shard_map/ppermute | solution.py:464
  44.1 5.6 %collective-permute-start.12 = (f32[16,8,128]{2,1,0:T(8,128)S(1)}, f32[16,8,128]{2,1,0:T(8,128)S(1)}, u32[]{:S(2)}, u32[]{:S(2)}) collective-permute-start(f32[16,8,128]{2,1,0:T(8,128)S(1)} %fusion.x0), channel_id=1, source_target_pairs={{0,16},{8,24},{16,0},{24,8},{1,17},{9,25},{17,1},{25,9},{2,18},{10... | collective-permute-start | bytes 196616 | tf_op jit(solution)/shard_map/ppermute | solution.py:464
  44.1 5.6 %collective-permute-start.11 = (f32[16,8,128]{2,1,0:T(8,128)S(1)}, f32[16,8,128]{2,1,0:T(8,128)S(1)}, u32[]{:S(2)}, u32[]{:S(2)}) collective-permute-start(f32[16,8,128]{2,1,0:T(8,128)S(1)} %fusion.x0), channel_id=1, source_target_pairs={{0,8},{8,0},{16,24},{24,16},{1,9},{9,1},{17,25},{25,17},{2,10},{10... | collective-permute-start | bytes 196616 | tf_op jit(solution)/shard_map/ppermute | solution.py:464
  47.6 2.1 %copy-start.3 = (f32[16,8,128]{2,1,0:T(8,128)}, f32[16,8,128]{2,1,0:T(8,128)S(1)}, u32[]{:S(2)}) copy-start(f32[16,8,128]{2,1,0:T(8,128)S(1)} %collective-permute-done.13.x3) | copy-start | bytes 196612
  49.8 0.6 %copy-start.4 = (f32[16,8,128]{2,1,0:T(8,128)}, f32[16,8,128]{2,1,0:T(8,128)S(1)}, u32[]{:S(2)}) copy-start(f32[16,8,128]{2,1,0:T(8,128)S(1)} %collective-permute-done.12.x2) | copy-start | bytes 196612
  49.8 0.6 %copy-start.5 = (f32[16,8,128]{2,1,0:T(8,128)}, f32[16,8,128]{2,1,0:T(8,128)S(1)}, u32[]{:S(2)}) copy-start(f32[16,8,128]{2,1,0:T(8,128)S(1)} %collective-permute-done.11.x1) | copy-start | bytes 196612
where the time goes:
time: 53.2 us; the launch traced here: 52.8 us
  waiting for transfers between devices  18.4 us (35%)
  starting transfers between devices  17.7 us (33%)
  Pallas kernels  9.92 us (19%)
  local copies, waits for them, and re-layouts  4.16 us (8%)
  other arithmetic  1.93 us (4%)
  between operations  0.71 us (1%)
    ppermute x14, waiting for transfers between devices, swap(): return lax.ppermute(x, axis, [(i, i ^ mask) for i in range(size)])  18.4 us
    ppermute x14, starting transfers between devices, swap(): return lax.ppermute(x, axis, [(i, i ^ mask) for i in range(size)])  17.7 us
    pallas_call x1, Pallas kernels, fast_device(): pl.pallas_call(functools.partial(image_kernel, shards=shards, scale=1.0 /...  4.65 us
    pallas_call x1, Pallas kernels, fast_device(): pl.pallas_call(functools.partial(grid_kernel, shards=shards, row_tiles=fa...  2.9 us
    unnamed x13, local copies, waits for them, and re-layouts  2.66 us
    pallas_call x1, Pallas kernels, fast_device(): pl.pallas_call(functools.partial(predict_kernel, scale=4.0 / SG / SG / fa...  2.37 us
    squeeze x1, local copies, waits for them, and re-layouts, fast_device(): lax.dynamic_index_in_dim(jnp.asarray(column_table(facet_len, rows)), bloc...  1.49 us
  transfers between devices with their start and end apart: 14, of which 10 were waited for; matrix products, arithmetic and copies ran while one was open for 3% of the time, Pallas kernels for 0%

commit v1 on v0

--- a/solution.py
+++ b/solution.py
@@ -262,17 +262,14 @@
 
 
 def grid_kernel(
-    row_ref, col_ref, vis_ref, uv_ref, chan_ref, counts_ref, window_ref, out_ref, a_ref, b_ref,
+    row_ref, col_ref, counts_ref, vis_ref, uv_ref, chan_ref, window_ref, out_ref, a_ref, b_ref,
     *, shards, row_tiles
 ):
     shard = lax.axis_index("chan")
     owner = lax.axis_index("sub")
     chan = (shard * CH_DEV + chan_ref[...]).astype(jnp.float32)
     scale = 1.0 + 0.5 * chan / (shards * CH_DEV)
-    slot = lax.broadcasted_iota(jnp.int32, (SUB_DEV, CAP), 1)
-    live = (slot < counts_ref[...]).astype(jnp.float32)
-    vis_re = vis_ref[0] * live
-    vis_im = vis_ref[1] * live
+    slot = lax.broadcasted_iota(jnp.int32, (1, CAP), 1)
     window = halves(window_ref[...])
     steps = lax.broadcasted_iota(jnp.int32, (8, CAP), 0).astype(jnp.float32) / SG
     far = []
@@ -295,7 +292,8 @@
         hat = dot3(window, halves(jnp.concatenate([b_re, b_im], axis=0)), NN)
         b_ref[j] = hat
         hat_re, hat_im = hat[:SG], hat[SG:]
-        re, im = vis_re[j : j + 1], vis_im[j : j + 1]
+        live = jnp.where(slot < counts_ref[j], 1.0, 0.0)
+        re, im = vis_ref[0, j : j + 1] * live, vis_ref[1, j : j + 1] * live
         left = jnp.concatenate([re * hat_re - im * hat_im, re * hat_im + im * hat_re], axis=1)
         right = jnp.concatenate(
             [jnp.concatenate([a_re, -a_im], axis=1), jnp.concatenate([a_im, a_re], axis=1)], axis=0
@@ -348,9 +346,15 @@
 
 
 def image_kernel(
-    own_ref, pair_ref, table_ref, beam_ref, model_ref, new_ref, own_out, pair_out,
-    wide_ref, spec_ref, back_ref, *, shards, scale
+    own_ref, pair_ref, table_ref, beam_hbm, model_hbm, new_hbm, own_out, pair_out,
+    wide_ref, spec_ref, back_ref, beam_ref, model_ref, new_ref, sems, *, shards, scale
 ):
+    loads = [
+        pltpu.make_async_copy(beam_hbm, beam_ref, sems.at[0]),
+        pltpu.make_async_copy(model_hbm, model_ref, sems.at[1]),
+    ]
+    for load in loads:
+        load.start()
     own_blocks = own_ref.shape[0]
     blocks = [own_ref.at[t] for t in range(own_blocks)] + [pair_ref.at[t] for t in range(own_blocks)]
     rows = beam_ref.shape[0]
@@ -392,6 +396,8 @@
         spec_ref[at] = dot3((wide_ref[0, at], wide_ref[1, at]), mix, NN)
     twist = [cis(lax.broadcasted_iota(jnp.int32, (8, LANES), 1).astype(jnp.float32) * (a / (RADIX * LANES))) for a in range(1, RADIX)]
 
+    for load in loads:
+        load.wait()
     for tile in range(rows // 8):
         at = lambda a: pl.ds(a * rows + tile * 8, 8)
         re = [spec_ref[at(0), :LANES]]
@@ -423,6 +429,8 @@
             x, y = (re[a], im[a]) if a < 8 else (re[RADIX - a], -im[RADIX - a])
             back_ref[at(a), :LANES] = x * c - y * s
             back_ref[at(a), LANES:] = -(x * s + y * c)
+    store = pltpu.make_async_copy(new_ref, new_hbm, sems.at[2])
+    store.start()
     for g in range(RADIX // 4):
         at = pl.ds(g * group, group)
         spec_ref[at] = dot3(halves(back_ref[at]), mix, NT)
@@ -440,9 +448,10 @@
                 own_out[t, h * RADIX // 2 + k] = part[first : first + SUB_DEV]
                 first += own_blocks * SUB_DEV
                 pair_out[t, h * RADIX // 2 + k] = part[first : first + SUB_DEV]
-
-
-def predict_kernel(x0, x1, x2, x3, a_ref, b_ref, counts_ref, out_ref, *, scale):
+    store.wait()
+
+
+def predict_kernel(counts_ref, x0, x1, x2, x3, a_ref, b_ref, out_ref, *, scale):
     total = (x0[...] + x1[...]) + (x2[...] + x3[...])
     slot = lax.broadcasted_iota(jnp.int32, (1, CAP), 1)
     for j in range(SUB_DEV):
@@ -452,7 +461,7 @@
         inner_re = dot3(left, halves(jnp.concatenate([a_re, a_im], axis=0)), NN)
         inner_im = dot3(left, halves(jnp.concatenate([-a_im, a_re], axis=0)), NN)
         b_re, b_im = b_ref[j, :SG], b_ref[j, SG:]
-        factor = jnp.where(slot < counts_ref[j : j + 1], scale, 0.0)
+        factor = jnp.where(slot < counts_ref[j], scale, 0.0)
         re = jnp.sum(b_re * inner_re + b_im * inner_im, axis=0, keepdims=True)
         im = jnp.sum(b_re * inner_im - b_im * inner_re, axis=0, keepdims=True)
         out_ref[0, j : j + 1] = re * factor
@@ -473,50 +482,56 @@
     f32 = jnp.float32
     vmem = pl.BlockSpec(memory_space=pltpu.VMEM)
     smem = pl.BlockSpec(memory_space=pltpu.SMEM)
-    shape = jax.ShapeDtypeStruct
+    hbm = pl.BlockSpec(memory_space=pl.ANY)
+    keep = lambda x: pltpu.with_memory_space_constraint(x, pltpu.VMEM)
+    counts = counts.reshape(SUB_DEV)
     payload, a_rows, b_rows = pl.pallas_call(
         functools.partial(grid_kernel, shards=shards, row_tiles=facet_len // owners // SG),
         out_shape=(
-            shape((RADIX + 1, SUB_DEV, LANES), f32),
-            shape((SUB_DEV, 2 * SG, CAP), f32),
-            shape((SUB_DEV, 2 * SG, CAP), f32),
+            pltpu.VMEM((RADIX + 1, SUB_DEV, LANES), f32),
+            pltpu.VMEM((SUB_DEV, 2 * SG, CAP), f32),
+            pltpu.VMEM((SUB_DEV, 2 * SG, CAP), f32),
         ),
-        in_specs=[smem, smem] + [vmem] * 5,
+        in_specs=[smem] * 3 + [vmem] * 4,
         out_specs=[vmem] * 3,
         name="grid",
-    )(row_tile, col_tile, visibilities, uv_offset, chan_index, counts, window_table())
+    )(row_tile, col_tile, counts, visibilities, uv_offset, chan_index, window_table())
     block = lax.axis_index("chan") * owners + lax.axis_index("sub")
     table = lax.dynamic_index_in_dim(jnp.asarray(column_table(facet_len, rows)), block, 0, False)
     payload = payload + sum(swap(payload, "chan", k) for k in range(1, shards))
     own = jnp.stack([payload] + [swap(payload, "sub", k) for k in range(2, owners, 2)])
     pair = swap(own, "sub", 1)
-    part = shape((owners // 2, RADIX, SUB_DEV, LANES), f32)
+    part = pltpu.VMEM((owners // 2, RADIX, SUB_DEV, LANES), f32)
     new_model, own, pair = pl.pallas_call(
         functools.partial(
             image_kernel,
             shards=shards,
             scale=1.0 / (SG * SG * math.sqrt(SUB_DEV * owners * CAP * shards)),
         ),
-        out_shape=(shape((rows, facet_len), f32), part, part),
-        in_specs=[vmem] * 5,
-        out_specs=[vmem] * 3,
+        out_shape=(jax.ShapeDtypeStruct((rows, facet_len), f32), part, part),
+        in_specs=[vmem] * 3 + [hbm] * 2,
+        out_specs=[hbm, vmem, vmem],
         scratch_shapes=[
             pltpu.VMEM((2, RADIX * rows, 2 * LANES), jnp.bfloat16),
             pltpu.VMEM((RADIX * rows, 2 * LANES), f32),
             pltpu.VMEM((RADIX * rows, 2 * LANES), f32),
+            pltpu.VMEM((rows, facet_len), f32),
+            pltpu.VMEM((rows, facet_len), f32),
+            pltpu.VMEM((rows, facet_len), f32),
+            pltpu.SemaphoreType.DMA((3,)),
         ],
         name="image",
-    )(own, pair, table, primary_beam, model_image)
+    )(keep(own), keep(pair), keep(table), primary_beam, model_image)
     own = own + swap(pair, "sub", 1)
     part = own[0] + sum(swap(own[k // 2], "sub", k) for k in range(2, owners, 2))
     parts = [part] + [swap(part, "chan", k) for k in range(1, shards)]
     predicted = pl.pallas_call(
         functools.partial(predict_kernel, scale=4.0 / SG / SG / facet_len),
-        out_shape=shape((2, SUB_DEV, CAP), f32),
-        in_specs=[vmem] * 7,
+        out_shape=jax.ShapeDtypeStruct((2, SUB_DEV, CAP), f32),
+        in_specs=[smem] + [vmem] * 6,
         out_specs=vmem,
         name="predict",
-    )(*parts, a_rows, b_rows, counts)
+    )(counts, *map(keep, parts), keep(a_rows), keep(b_rows))
     return new_model, predicted
 
 

time: 53.2 us -> 45 us (0.85)
  local copies, waits for them, and re-layouts: 4.16 us -> 0.87 us
  Pallas kernels: 9.92 us -> 7.07 us
  other arithmetic: 1.93 us -> 0.11 us
    unnamed x13 -> x0, local copies, waits for them, and re-layouts: 2.66 us -> none
    pallas_call x1, Pallas kernels: 4.65 us -> 3.09 us  [fast_device(): pl.pallas_call(functools.partial(image_kernel, shards=shards, scale=1.0 /...]
    add x1, other arithmetic: 0.99 us -> 0.05 us  [fast_device(): own = own + swap(pair, 'sub', 1)]
    add x1, other arithmetic: 0.9 us -> 0.02 us  [fast_device(): payload + sum((swap(payload, 'chan', k) for k in range(1, shards)))]
    pallas_call x1, Pallas kernels: 2.37 us -> 1.72 us  [fast_device(): pl.pallas_call(functools.partial(predict_kernel, scale=4.0 / SG / SG / fa...]
    squeeze x1, local copies, waits for them, and re-layouts: 1.49 us -> 0.85 us  [fast_device(): lax.dynamic_index_in_dim(jnp.asarray(column_table(facet_len, rows)), bloc...]
    pallas_call x1, Pallas kernels: 2.9 us -> 2.27 us  [fast_device(): pl.pallas_call(functools.partial(grid_kernel, shards=shards, row_tiles=fa...]
  transfers between devices with their start and end apart: 14 -> 14, of which waited for: 10 -> 11; matrix products, arithmetic and copies ran while one was open for 3% -> 2% of each run, Pallas kernels for 0% -> 0%
where the time goes in v1:
time: 45 us; the launch traced here: 44.8 us
  waiting for transfers between devices  18.4 us (41%)
  starting transfers between devices  17.6 us (39%)
  Pallas kernels  7.07 us (16%)
  local copies, waits for them, and re-layouts  0.87 us (2%)
  between operations  0.69 us (2%)
    ppermute x14, waiting for transfers between devices, swap(): return lax.ppermute(x, axis, [(i, i ^ mask) for i in range(size)])  18.4 us
    ppermute x14, starting transfers between devices, swap(): return lax.ppermute(x, axis, [(i, i ^ mask) for i in range(size)])  17.6 us
    pallas_call x1, Pallas kernels, fast_device(): pl.pallas_call(functools.partial(image_kernel, shards=shards, scale=1.0 /...  3.09 us
    pallas_call x1, Pallas kernels, fast_device(): pl.pallas_call(functools.partial(grid_kernel, shards=shards, row_tiles=fa...  2.27 us
    pallas_call x1, Pallas kernels, fast_device(): pl.pallas_call(functools.partial(predict_kernel, scale=4.0 / SG / SG / fa...  1.72 us
  transfers between devices with their start and end apart: 14, of which 11 were waited for; matrix products, arithmetic and copies ran while one was open for 2% of the time, Pallas kernels for 0%

profile of v1, /device:TPU:0, one launch (start us, length us, event | category | flops | bytes accessed | tf_op | source)
XLA Modules:
  0.0 44.8 jit_solution(13723636261316426896)
XLA Ops:
  0.6 2.3 %grid.1 = (f32[17,8,128]{2,1,0:T(8,128)S(1)}, f32[8,64,256]{2,1,0:T(8,128)S(1)}, f32[8,64,256]{2,1,0:T(8,128)S(1)}) custom-call(s32[8]{0:T(128)} %row_ref.1, s32[8]{0:T(128)} %col_ref.1, s32[8]{0:T(128)} %bitcast.21, f32[2,8,256]{2,1,0:T(8,128)} %vis_ref.1, f32[2,8,256]{2,1,0:T(8,128)} %uv_ref.1, s32[8,256]{1,0:T(8,128)} %chan_ref.1, ...), custom_call_target="tpu_custom_call" | custom-call | tf_op jit(solution)/shard_map/grid/pallas_call | solution.py:488
  2.9 5.1 %collective-permute-start.2 = (f32[17,8,128]{2,1,0:T(8,128)S(1)}, f32[17,8,128]{2,1,0:T(8,128)S(1)}, u32[]{:S(2)}, u32[]{:S(2)}) collective-permute-start(f32[17,8,128]{2,1,0:T(8,128)S(1)} %get-tuple-element.8), channel_id=1, source_target_pairs={{0,24},{8,16},{16,8},{24,0},{1,25},{9,17},{17,9},{25,1},{2,26},{10... | collective-permute-start | bytes 208904 | tf_op jit(solution)/shard_map/ppermute | solution.py:473
  8.0 0.0 collective-permute-start.1
  8.0 0.6 %collective-permute-start = (f32[17,8,128]{2,1,0:T(8,128)S(1)}, f32[17,8,128]{2,1,0:T(8,128)S(1)}, u32[]{:S(2)}, u32[]{:S(2)}) collective-permute-start(f32[17,8,128]{2,1,0:T(8,128)S(1)} %get-tuple-element.8), channel_id=1, source_target_pairs={{0,8},{8,0},{16,24},{24,16},{1,9},{9,1},{17,25},{25,17},{2,10},{10... | collective-permute-start | bytes 208904 | tf_op jit(solution)/shard_map/ppermute | solution.py:473
  8.7 1.9 %collective-permute-done.2 = f32[17,8,128]{2,1,0:T(8,128)S(1)} collective-permute-done((f32[17,8,128]{2,1,0:T(8,128)S(1)}, f32[17,8,128]{2,1,0:T(8,128)S(1)}, u32[]{:S(2)}, u32[]{:S(2)}) %collective-permute-start.2) | collective-permute-done | bytes 69664 | tf_op jit(solution)/shard_map/ppermute | solution.py:473
  10.6 3.3 %collective-permute-done.1 = f32[17,8,128]{2,1,0:T(8,128)S(1)} collective-permute-done((f32[17,8,128]{2,1,0:T(8,128)S(1)}, f32[17,8,128]{2,1,0:T(8,128)S(1)}, u32[]{:S(2)}, u32[]{:S(2)}) %collective-permute-start.1) | collective-permute-done | bytes 69664 | tf_op jit(solution)/shard_map/ppermute | solution.py:473
  14.0 0.0 collective-permute-done
  14.0 2.5 %collective-permute-start.5 = (f32[17,8,128]{2,1,0:T(8,128)S(1)}, f32[17,8,128]{2,1,0:T(8,128)S(1)}, u32[]{:S(2)}, u32[]{:S(2)}) collective-permute-start(f32[17,8,128]{2,1,0:T(8,128)S(1)} %add_add_fusion), channel_id=1, source_target_pairs={{0,6},{1,7},{2,4},{3,5},{4,2},{5,3},{6,0},{7,1},{8,14},{9,15},{10,... | collective-permute-start | bytes 208904 | tf_op jit(solution)/shard_map/ppermute | solution.py:473
  16.5 0.5 %collective-permute-start.4 = (f32[17,8,128]{2,1,0:T(8,128)S(1)}, f32[17,8,128]{2,1,0:T(8,128)S(1)}, u32[]{:S(2)}, u32[]{:S(2)}) collective-permute-start(f32[17,8,128]{2,1,0:T(8,128)S(1)} %add_add_fusion), channel_id=1, source_target_pairs={{0,4},{1,5},{2,6},{3,7},{4,0},{5,1},{6,2},{7,3},{8,12},{9,13},{10,... | collective-permute-start | bytes 208904 | tf_op jit(solution)/shard_map/ppermute | solution.py:473
  17.0 0.5 %collective-permute-start.3 = (f32[17,8,128]{2,1,0:T(8,128)S(1)}, f32[17,8,128]{2,1,0:T(8,128)S(1)}, u32[]{:S(2)}, u32[]{:S(2)}) collective-permute-start(f32[17,8,128]{2,1,0:T(8,128)S(1)} %add_add_fusion), channel_id=1, source_target_pairs={{0,2},{1,3},{2,0},{3,1},{4,6},{5,7},{6,4},{7,5},{8,10},{9,11},{10,... | collective-permute-start | bytes 208904 | tf_op jit(solution)/shard_map/ppermute | solution.py:473
  17.5 1.8 %collective-permute-done.5 = f32[17,8,128]{2,1,0:T(8,128)S(1)} collective-permute-done((f32[17,8,128]{2,1,0:T(8,128)S(1)}, f32[17,8,128]{2,1,0:T(8,128)S(1)}, u32[]{:S(2)}, u32[]{:S(2)}) %collective-permute-start.5) | collective-permute-done | bytes 69664 | tf_op jit(solution)/shard_map/ppermute | solution.py:473
  19.4 1.4 %collective-permute-done.4 = f32[17,8,128]{2,1,0:T(8,128)S(1)} collective-permute-done((f32[17,8,128]{2,1,0:T(8,128)S(1)}, f32[17,8,128]{2,1,0:T(8,128)S(1)}, u32[]{:S(2)}, u32[]{:S(2)}) %collective-permute-start.4) | collective-permute-done | bytes 69664 | tf_op jit(solution)/shard_map/ppermute | solution.py:473
  20.8 0.5 %collective-permute-done.3 = f32[17,8,128]{2,1,0:T(8,128)S(1)} collective-permute-done((f32[17,8,128]{2,1,0:T(8,128)S(1)}, f32[17,8,128]{2,1,0:T(8,128)S(1)}, u32[]{:S(2)}, u32[]{:S(2)}) %collective-permute-start.3) | collective-permute-done | bytes 69664 | tf_op jit(solution)/shard_map/ppermute | solution.py:473
  21.3 0.1 collective-permute-start.6
  21.4 0.9 %dynamic-slice_bitcast_fusion.table_ref = f32[128,64]{1,0:T(8,128)S(1)} fusion(f32[32,128,64]{2,1,0:T(8,128)} %constant.21.clone, s32[]{:T(128)S(6)} %select_n.4), kind=kLoop, calls=%fused_computation.7 | loop fusion | bytes 65540 | tf_op jit(solution)/shard_map/jit(dynamic_index_in_dim)/squeeze | solution.py:500
  22.3 0.7 %collective-permute-done.6.pair_ref = f32[4,17,8,128]{3,2,1,0:T(8,128)S(1)} collective-permute-done((f32[4,17,8,128]{3,2,1,0:T(8,128)S(1)}, f32[4,17,8,128]{3,2,1,0:T(8,128)S(1)}, u32[]{:S(2)}, u32[]{:S(2)}) %collective-permute-start.6) | collective-permute-done | bytes 278560 | tf_op jit(solution)/shard_map/ppermute | solution.py:473
  23.0 3.1 %image.1 = (f32[64,2048]{1,0:T(8,128)}, f32[4,16,8,128]{3,2,1,0:T(8,128)S(1)}, f32[4,16,8,128]{3,2,1,0:T(8,128)S(1)}) custom-call(f32[4,17,8,128]{3,2,1,0:T(8,128)S(1)} %pad_maximum_fusion.own_ref, f32[4,17,8,128]{3,2,1,0:T(8,128)S(1)} %collective-permute-done.6.pair_ref, f32[128,64]{1,0:T(8,128)S(1)} %dynamic-slice_bitcast_fusion.table_ref, ...), custom_call_target="tpu_custom_call" | custom-call | tf_op jit(solution)/shard_map/image/pallas_call | solution.py:505
  26.1 0.2 collective-permute-start.7
  26.3 1.4 %collective-permute-done.7 = f32[4,16,8,128]{3,2,1,0:T(8,128)S(1)} collective-permute-done((f32[4,16,8,128]{3,2,1,0:T(8,128)S(1)}, f32[4,16,8,128]{3,2,1,0:T(8,128)S(1)}, u32[]{:S(2)}, u32[]{:S(2)}) %collective-permute-start.7) | collective-permute-done | bytes 262176 | tf_op jit(solution)/shard_map/ppermute | solution.py:473
  27.7 1.6 %collective-permute-start.9 = (f32[16,8,128]{2,1,0:T(8,128)S(1)}, f32[16,8,128]{2,1,0:T(8,128)S(1)}, u32[]{:S(2)}, u32[]{:S(2)}) collective-permute-start(f32[16,8,128]{2,1,0:T(8,128)S(1)} %get-tuple-element.14), channel_id=1, source_target_pairs={{0,4},{1,5},{2,6},{3,7},{4,0},{5,1},{6,2},{7,3},{8,12},{9,13},{10,... | collective-permute-start | bytes 196616 | tf_op jit(solution)/shard_map/ppermute | solution.py:473
  29.3 0.5 %collective-permute-start.10 = (f32[16,8,128]{2,1,0:T(8,128)S(1)}, f32[16,8,128]{2,1,0:T(8,128)S(1)}, u32[]{:S(2)}, u32[]{:S(2)}) collective-permute-start(f32[16,8,128]{2,1,0:T(8,128)S(1)} %get-tuple-element.15), channel_id=1, source_target_pairs={{0,6},{1,7},{2,4},{3,5},{4,2},{5,3},{6,0},{7,1},{8,14},{9,15},{10,... | collective-permute-start | bytes 196616 | tf_op jit(solution)/shard_map/ppermute | solution.py:473
  29.8 1.5 %collective-permute-start.8 = (f32[16,8,128]{2,1,0:T(8,128)S(1)}, f32[16,8,128]{2,1,0:T(8,128)S(1)}, u32[]{:S(2)}, u32[]{:S(2)}) collective-permute-start(f32[16,8,128]{2,1,0:T(8,128)S(1)} %get-tuple-element.16), channel_id=1, source_target_pairs={{0,2},{1,3},{2,0},{3,1},{4,6},{5,7},{6,4},{7,5},{8,10},{9,11},{10,... | collective-permute-start | bytes 196616 | tf_op jit(solution)/shard_map/ppermute | solution.py:473
  31.3 0.8 %collective-permute-done.9 = f32[16,8,128]{2,1,0:T(8,128)S(1)} collective-permute-done((f32[16,8,128]{2,1,0:T(8,128)S(1)}, f32[16,8,128]{2,1,0:T(8,128)S(1)}, u32[]{:S(2)}, u32[]{:S(2)}) %collective-permute-start.9) | collective-permute-done | bytes 65568 | tf_op jit(solution)/shard_map/ppermute | solution.py:473
  32.1 2.7 %collective-permute-done.10 = f32[16,8,128]{2,1,0:T(8,128)S(1)} collective-permute-done((f32[16,8,128]{2,1,0:T(8,128)S(1)}, f32[16,8,128]{2,1,0:T(8,128)S(1)}, u32[]{:S(2)}, u32[]{:S(2)}) %collective-permute-start.10) | collective-permute-done | bytes 65568 | tf_op jit(solution)/shard_map/ppermute | solution.py:473
  34.8 0.0 collective-permute-done.8
  34.8 2.8 %collective-permute-start.13 = (f32[16,8,128]{2,1,0:T(8,128)S(1)}, f32[16,8,128]{2,1,0:T(8,128)S(1)}, u32[]{:S(2)}, u32[]{:S(2)}) collective-permute-start(f32[16,8,128]{2,1,0:T(8,128)S(1)} %fusion.x0), channel_id=1, source_target_pairs={{0,24},{8,16},{16,8},{24,0},{1,25},{9,17},{17,9},{25,1},{2,26},{10... | collective-permute-start | bytes 196616 | tf_op jit(solution)/shard_map/ppermute | solution.py:473
  37.6 0.0 collective-permute-start.12
  37.6 1.7 %collective-permute-start.11 = (f32[16,8,128]{2,1,0:T(8,128)S(1)}, f32[16,8,128]{2,1,0:T(8,128)S(1)}, u32[]{:S(2)}, u32[]{:S(2)}) collective-permute-start(f32[16,8,128]{2,1,0:T(8,128)S(1)} %fusion.x0), channel_id=1, source_target_pairs={{0,8},{8,0},{16,24},{24,16},{1,9},{9,1},{17,25},{25,17},{2,10},{10... | collective-permute-start | bytes 196616 | tf_op jit(solution)/shard_map/ppermute | solution.py:473
  39.2 2.2 %collective-permute-done.13.x3 = f32[16,8,128]{2,1,0:T(8,128)S(1)} collective-permute-done((f32[16,8,128]{2,1,0:T(8,128)S(1)}, f32[16,8,128]{2,1,0:T(8,128)S(1)}, u32[]{:S(2)}, u32[]{:S(2)}) %collective-permute-start.13) | collective-permute-done | bytes 65568 | tf_op jit(solution)/shard_map/ppermute | solution.py:473
  41.4 1.6 %collective-permute-done.12.x2 = f32[16,8,128]{2,1,0:T(8,128)S(1)} collective-permute-done((f32[16,8,128]{2,1,0:T(8,128)S(1)}, f32[16,8,128]{2,1,0:T(8,128)S(1)}, u32[]{:S(2)}, u32[]{:S(2)}) %collective-permute-start.12) | collective-permute-done | bytes 65568 | tf_op jit(solution)/shard_map/ppermute | solution.py:473
  43.0 0.0 collective-permute-done.11.x1
  43.0 1.7 %predict.1 = f32[2,8,256]{2,1,0:T(8,128)} custom-call(s32[8]{0:T(128)} %bitcast.22, f32[16,8,128]{2,1,0:T(8,128)S(1)} %fusion.x0, f32[16,8,128]{2,1,0:T(8,128)S(1)} %collective-permute-done.11.x1, f32[16,8,128]{2,1,0:T(8,128)S(1)} %collective-permute-done.12.x2, f32[16,8,128]{2,1,0:T(8,128)S(1)} %collective-permute-done.13.x3, ...), custom_call_target="tpu_custom_call" | custom-call | tf_op jit(solution)/shard_map/predict/pallas_call | solution.py:528
  (5 shorter events, 0.1 us)
Async XLA Ops:
  2.9 7.7 %collective-permute-start.2 = (f32[17,8,128]{2,1,0:T(8,128)S(1)}, f32[17,8,128]{2,1,0:T(8,128)S(1)}, u32[]{:S(2)}, u32[]{:S(2)}) collective-permute-start(f32[17,8,128]{2,1,0:T(8,128)S(1)} %get-tuple-element.8), channel_id=1, source_target_pairs={{0,24},{8,16},{16,8},{24,0},{1,25},{9,17},{17,9},{25,1},{2,26},{10... | collective-permute-start | bytes 208904 | tf_op jit(solution)/shard_map/ppermute | solution.py:473
  8.0 5.9 %collective-permute-start.1 = (f32[17,8,128]{2,1,0:T(8,128)S(1)}, f32[17,8,128]{2,1,0:T(8,128)S(1)}, u32[]{:S(2)}, u32[]{:S(2)}) collective-permute-start(f32[17,8,128]{2,1,0:T(8,128)S(1)} %get-tuple-element.8), channel_id=1, source_target_pairs={{0,16},{8,24},{16,0},{24,8},{1,17},{9,25},{17,1},{25,9},{2,18},{10... | collective-permute-start | bytes 208904 | tf_op jit(solution)/shard_map/ppermute | solution.py:473
  8.0 5.9 %collective-permute-start = (f32[17,8,128]{2,1,0:T(8,128)S(1)}, f32[17,8,128]{2,1,0:T(8,128)S(1)}, u32[]{:S(2)}, u32[]{:S(2)}) collective-permute-start(f32[17,8,128]{2,1,0:T(8,128)S(1)} %get-tuple-element.8), channel_id=1, source_target_pairs={{0,8},{8,0},{16,24},{24,16},{1,9},{9,1},{17,25},{25,17},{2,10},{10... | collective-permute-start | bytes 208904 | tf_op jit(solution)/shard_map/ppermute | solution.py:473
  14.0 5.4 %collective-permute-start.5 = (f32[17,8,128]{2,1,0:T(8,128)S(1)}, f32[17,8,128]{2,1,0:T(8,128)S(1)}, u32[]{:S(2)}, u32[]{:S(2)}) collective-permute-start(f32[17,8,128]{2,1,0:T(8,128)S(1)} %add_add_fusion), channel_id=1, source_target_pairs={{0,6},{1,7},{2,4},{3,5},{4,2},{5,3},{6,0},{7,1},{8,14},{9,15},{10,... | collective-permute-start | bytes 208904 | tf_op jit(solution)/shard_map/ppermute | solution.py:473
  16.5 4.3 %collective-permute-start.4 = (f32[17,8,128]{2,1,0:T(8,128)S(1)}, f32[17,8,128]{2,1,0:T(8,128)S(1)}, u32[]{:S(2)}, u32[]{:S(2)}) collective-permute-start(f32[17,8,128]{2,1,0:T(8,128)S(1)} %add_add_fusion), channel_id=1, source_target_pairs={{0,4},{1,5},{2,6},{3,7},{4,0},{5,1},{6,2},{7,3},{8,12},{9,13},{10,... | collective-permute-start | bytes 208904 | tf_op jit(solution)/shard_map/ppermute | solution.py:473
  17.0 4.3 %collective-permute-start.3 = (f32[17,8,128]{2,1,0:T(8,128)S(1)}, f32[17,8,128]{2,1,0:T(8,128)S(1)}, u32[]{:S(2)}, u32[]{:S(2)}) collective-permute-start(f32[17,8,128]{2,1,0:T(8,128)S(1)} %add_add_fusion), channel_id=1, source_target_pairs={{0,2},{1,3},{2,0},{3,1},{4,6},{5,7},{6,4},{7,5},{8,10},{9,11},{10,... | collective-permute-start | bytes 208904 | tf_op jit(solution)/shard_map/ppermute | solution.py:473
  21.3 1.6 %collective-permute-start.6 = (f32[4,17,8,128]{3,2,1,0:T(8,128)S(1)}, f32[4,17,8,128]{3,2,1,0:T(8,128)S(1)}, u32[]{:S(2)}, u32[]{:S(2)}) collective-permute-start(f32[4,17,8,128]{3,2,1,0:T(8,128)S(1)} %pad_maximum_fusion.own_ref), channel_id=1, source_target_pairs={{0,1},{1,0},{2,3},{3,2},{4,5},{5,4},{6,7},{7,6},{8,9},{9,8},{10,11... | collective-permute-start | bytes 835592 | tf_op jit(solution)/shard_map/ppermute | solution.py:473
  26.1 1.6 %collective-permute-start.7 = (f32[4,16,8,128]{3,2,1,0:T(8,128)S(1)}, f32[4,16,8,128]{3,2,1,0:T(8,128)S(1)}, u32[]{:S(2)}, u32[]{:S(2)}) collective-permute-start(f32[4,16,8,128]{3,2,1,0:T(8,128)S(1)} %get-tuple-element.11), channel_id=1, source_target_pairs={{0,1},{1,0},{2,3},{3,2},{4,5},{5,4},{6,7},{7,6},{8,9},{9,8},{10,11... | collective-permute-start | bytes 786440 | tf_op jit(solution)/shard_map/ppermute | solution.py:473
  27.7 4.3 %collective-permute-start.9 = (f32[16,8,128]{2,1,0:T(8,128)S(1)}, f32[16,8,128]{2,1,0:T(8,128)S(1)}, u32[]{:S(2)}, u32[]{:S(2)}) collective-permute-start(f32[16,8,128]{2,1,0:T(8,128)S(1)} %get-tuple-element.14), channel_id=1, source_target_pairs={{0,4},{1,5},{2,6},{3,7},{4,0},{5,1},{6,2},{7,3},{8,12},{9,13},{10,... | collective-permute-start | bytes 196616 | tf_op jit(solution)/shard_map/ppermute | solution.py:473
  29.3 5.5 %collective-permute-start.10 = (f32[16,8,128]{2,1,0:T(8,128)S(1)}, f32[16,8,128]{2,1,0:T(8,128)S(1)}, u32[]{:S(2)}, u32[]{:S(2)}) collective-permute-start(f32[16,8,128]{2,1,0:T(8,128)S(1)} %get-tuple-element.15), channel_id=1, source_target_pairs={{0,6},{1,7},{2,4},{3,5},{4,2},{5,3},{6,0},{7,1},{8,14},{9,15},{10,... | collective-permute-start | bytes 196616 | tf_op jit(solution)/shard_map/ppermute | solution.py:473
  29.8 5.0 %collective-permute-start.8 = (f32[16,8,128]{2,1,0:T(8,128)S(1)}, f32[16,8,128]{2,1,0:T(8,128)S(1)}, u32[]{:S(2)}, u32[]{:S(2)}) collective-permute-start(f32[16,8,128]{2,1,0:T(8,128)S(1)} %get-tuple-element.16), channel_id=1, source_target_pairs={{0,2},{1,3},{2,0},{3,1},{4,6},{5,7},{6,4},{7,5},{8,10},{9,11},{10,... | collective-permute-start | bytes 196616 | tf_op jit(solution)/shard_map/ppermute | solution.py:473
  34.8 6.6 %collective-permute-start.13 = (f32[16,8,128]{2,1,0:T(8,128)S(1)}, f32[16,8,128]{2,1,0:T(8,128)S(1)}, u32[]{:S(2)}, u32[]{:S(2)}) collective-permute-start(f32[16,8,128]{2,1,0:T(8,128)S(1)} %fusion.x0), channel_id=1, source_target_pairs={{0,24},{8,16},{16,8},{24,0},{1,25},{9,17},{17,9},{25,1},{2,26},{10... | collective-permute-start | bytes 196616 | tf_op jit(solution)/shard_map/ppermute | solution.py:473
  37.6 5.5 %collective-permute-start.12 = (f32[16,8,128]{2,1,0:T(8,128)S(1)}, f32[16,8,128]{2,1,0:T(8,128)S(1)}, u32[]{:S(2)}, u32[]{:S(2)}) collective-permute-start(f32[16,8,128]{2,1,0:T(8,128)S(1)} %fusion.x0), channel_id=1, source_target_pairs={{0,16},{8,24},{16,0},{24,8},{1,17},{9,25},{17,1},{25,9},{2,18},{10... | collective-permute-start | bytes 196616 | tf_op jit(solution)/shard_map/ppermute | solution.py:473
  37.6 5.5 %collective-permute-start.11 = (f32[16,8,128]{2,1,0:T(8,128)S(1)}, f32[16,8,128]{2,1,0:T(8,128)S(1)}, u32[]{:S(2)}, u32[]{:S(2)}) collective-permute-start(f32[16,8,128]{2,1,0:T(8,128)S(1)} %fusion.x0), channel_id=1, source_target_pairs={{0,8},{8,0},{16,24},{24,16},{1,9},{9,1},{17,25},{25,17},{2,10},{10... | collective-permute-start | bytes 196616 | tf_op jit(solution)/shard_map/ppermute | solution.py:473
